TPU v7x, 32 devices: a whole 2x2x4 slice. The times are simulated.
32 devices in a mesh: row: 4 (over x, core), col: 4 (over z), pt: 2 (over y).
Axes of the slice: x: 2, y: 2, z: 4, core: 2. Of those that a mesh axis runs over, the one named last changes fastest.
Arguments:
- first_factors: int32 [32, 1024, 1024], P('pt', 'row', 'col'), may hold values from 0 to 12288
- second_factors: int32 [32, 1024, 1024], P('pt', 'row', 'col'), may hold values from 0 to 12288
Outputs:
- scaled_product: float32 [45, 1024, 1024], P(None, ('row', 'pt'), 'col')
All inputs are finite; a program needn't handle non-finite values.
Results may differ from a plain program's by a relative error of at most 0.0003.
Values may be sent and summed in bfloat16 or wider, within the bound.
A program may use at most 128 MiB of HBM per device.

v0:
```python
import jax
import jax.numpy as jnp
import numpy as np
from jax import lax
from jax.sharding import PartitionSpec as P

DEG = 16
modulus = 12289
digit_base = 128


def primitive_root():
    for candidate in range(2, modulus):
        if pow(candidate, 6144, modulus) != 1 and pow(candidate, 4096, modulus) != 1:
            return candidate
    return 0


def make_table(order_size, row_count, column_count, inverse):
    generator = primitive_root()
    root_value = pow(generator, (modulus - 1) // order_size, modulus)
    scaling = 1
    if inverse:
        root_value = pow(root_value, modulus - 2, modulus)
        scaling = pow(order_size, modulus - 2, modulus)
    entries = [
        [
            pow(root_value, row_index * column_index % order_size, modulus) * scaling % modulus
            for column_index in range(column_count)
        ]
        for row_index in range(row_count)
    ]
    return np.array(entries, dtype=np.int64)


def value_digits(values):
    high_digit = values // digit_base
    return (
        high_digit.astype(jnp.bfloat16),
        (values - digit_base * high_digit).astype(jnp.bfloat16),
    )


def combine(high_high, high_low, low_high, low_low):
    top_part = high_high.astype(jnp.int32) % modulus
    middle_part = (high_low.astype(jnp.int32) + low_high.astype(jnp.int32)) % modulus
    return (
        top_part * (digit_base * digit_base) % modulus
        + middle_part * digit_base
        + low_low.astype(jnp.int32)
    ) % modulus


def transform(matrix_table, coefs):
    slot_count = coefs.shape[0]
    flat_coefs = coefs.reshape(slot_count, -1)
    table_high = jnp.asarray(matrix_table // digit_base, dtype=jnp.bfloat16)
    table_low = jnp.asarray(matrix_table % digit_base, dtype=jnp.bfloat16)
    data_high, data_low = value_digits(flat_coefs)

    def product_of(left_part, right_part):
        return jnp.dot(left_part, right_part, preferred_element_type=jnp.float32)

    mixed_values = combine(
        product_of(table_high, data_high),
        product_of(table_high, data_low),
        product_of(table_low, data_high),
        product_of(table_low, data_low),
    )
    return mixed_values.reshape(matrix_table.shape[0], coefs.shape[1], coefs.shape[2])


def batched_product(left_part, right_part):
    return jnp.einsum("bik,bkj->bij", left_part, right_part, preferred_element_type=jnp.float32)


def digit_sum(totals, left_digits, right_digits):
    return (
        totals[0] + batched_product(left_digits[0], right_digits[0]),
        totals[1] + batched_product(left_digits[0], right_digits[1]),
        totals[2] + batched_product(left_digits[1], right_digits[0]),
        totals[3] + batched_product(left_digits[1], right_digits[1]),
    )


def pointwise(left_values, right_values):
    left_points, right_points = (
        lax.all_to_all(
            lax.all_to_all(
                left_values.astype(jnp.float32), "col", split_axis=0, concat_axis=2, tiled=True
            ),
            "pt",
            split_axis=0,
            concat_axis=1,
            tiled=True,
        ),
        lax.all_to_all(
            lax.all_to_all(
                right_values.astype(jnp.float32), "col", split_axis=0, concat_axis=2, tiled=True
            ),
            "pt",
            split_axis=0,
            concat_axis=1,
            tiled=True,
        ),
    )
    left_digits = value_digits(left_points.astype(jnp.int32))
    right_digits = value_digits(right_points.astype(jnp.int32))
    zeros_init = jnp.zeros(left_points.shape, jnp.float32)
    column_parts = tuple((digit_part for digit_part in left_digits))
    totals = digit_sum(
        (zeros_init, zeros_init, zeros_init, zeros_init),
        column_parts,
        (
            lax.all_gather(right_digits[0], "row", axis=1, tiled=True),
            lax.all_gather(right_digits[1], "row", axis=1, tiled=True),
        ),
    )
    product_values = combine(totals[0], totals[1], totals[2], totals[3]).astype(jnp.float32)
    arrived = lax.all_to_all(
        lax.all_to_all(product_values, "col", split_axis=2, concat_axis=0, tiled=True),
        "pt",
        split_axis=1,
        concat_axis=0,
        tiled=True,
    )
    col_count = lax.axis_size("col")
    pt_count = lax.axis_size("pt")
    local_count = arrived.shape[0] // (col_count * pt_count)
    returned = arrived.reshape(pt_count, col_count, local_count, arrived.shape[1], arrived.shape[2])
    returned = returned.transpose(1, 0, 2, 3, 4).reshape(arrived.shape)
    return returned.astype(jnp.int32)


def local(first_factors, second_factors):
    forward_one = make_table(2 * DEG, 2 * DEG, DEG, False)
    inverse_one = make_table(2 * DEG, 2 * DEG, 2 * DEG, True)
    forward_two = make_table(4 * DEG, 4 * DEG, 2 * DEG, False)
    inverse_two = make_table(4 * DEG, 3 * DEG - 3, 4 * DEG, True)
    first_entries, second_entries = (
        lax.all_to_all(
            first_factors.astype(jnp.float32), "pt", split_axis=1, concat_axis=0, tiled=True
        ),
        lax.all_to_all(
            second_factors.astype(jnp.float32), "pt", split_axis=1, concat_axis=0, tiled=True
        ),
    )
    first_entries = first_entries.astype(jnp.int32)
    second_entries = second_entries.astype(jnp.int32)
    left_values = jnp.concatenate(
        [transform(forward_one, first_entries[:DEG]), transform(forward_one, first_entries[DEG:])],
        0,
    )
    right_values = jnp.concatenate(
        [
            transform(forward_one, second_entries[:DEG]),
            transform(forward_one, second_entries[DEG:]),
        ],
        0,
    )
    products = pointwise(left_values, right_values)
    first_product = transform(inverse_one, products[: 2 * DEG])
    second_product = transform(inverse_one, products[2 * DEG :])
    upper_values = transform(forward_two, first_product)
    lower_values = transform(forward_two[:, :DEG], second_product[DEG:])
    result_coefficients = transform(inverse_two, pointwise(upper_values, lower_values))
    return result_coefficients.astype(jnp.float32) / 12289.0


def reduce_centred(values):
    return values - 12289.0 * jnp.round(values * (1.0 / 12289.0))


def centred_digits(values):
    high_digit = jnp.round(values * (1.0 / 128.0))
    return (high_digit.astype(jnp.bfloat16), (values - 128.0 * high_digit).astype(jnp.bfloat16))


def combine_centred(high_high, middle, low_low):
    upper_part = reduce_centred(reduce_centred(high_high) * 128.0 + middle)
    return reduce_centred(upper_part * 128.0 + low_low)


def table_digits(matrix_table):
    centred = np.where(matrix_table > modulus // 2, matrix_table - modulus, matrix_table)
    high_digit = np.round(centred / 128.0)
    return (high_digit, centred - 128.0 * high_digit)


def centred_transform(table_high, table_low, coefs):
    data_high, data_low = centred_digits(coefs.astype(jnp.float32))
    table_high = jnp.asarray(table_high, dtype=jnp.bfloat16)
    table_low = jnp.asarray(table_low, dtype=jnp.bfloat16)

    def product_of(left_part, right_part):
        return jnp.einsum("ts,sab->tab", left_part, right_part, preferred_element_type=jnp.float32)

    middle = product_of(
        jnp.concatenate([table_high, table_low], 1), jnp.concatenate([data_low, data_high], 0)
    )
    return combine_centred(
        product_of(table_high, data_high), middle, product_of(table_low, data_low)
    )


def column_pointwise(left_values, right_values):
    right_points = lax.all_to_all(
        right_values.astype(jnp.int16), "col", split_axis=0, concat_axis=2, tiled=True
    )
    right_points = lax.all_gather(right_points, "row", axis=1, tiled=True)
    left_points = lax.all_to_all(
        left_values.astype(jnp.int16), "col", split_axis=0, concat_axis=2, tiled=True
    )
    left_high, left_low = centred_digits(left_points.astype(jnp.float32))
    right_high, right_low = centred_digits(right_points.astype(jnp.float32))
    middle = batched_product(left_high, right_low) + batched_product(left_low, right_high)
    product_values = combine_centred(
        batched_product(left_high, right_high), middle, batched_product(left_low, right_low)
    )
    return lax.all_to_all(
        product_values.astype(jnp.int16), "col", split_axis=2, concat_axis=0, tiled=True
    )


def pair_local(first_factors, second_factors):
    forward_one = table_digits(make_table(2 * DEG, 2 * DEG, DEG, False))
    inverse_one = table_digits(make_table(2 * DEG, 2 * DEG, 2 * DEG, True))
    forward_two = table_digits(make_table(4 * DEG, 4 * DEG, 2 * DEG, False))
    inverse_two = table_digits(make_table(4 * DEG, 3 * DEG - 3, 4 * DEG, True))
    half_points = 2 * DEG
    place = lax.axis_index("pt")
    products = column_pointwise(
        centred_transform(*forward_one, centre(first_factors)),
        centred_transform(*forward_one, centre(second_factors)),
    )
    own_product = centred_transform(*inverse_one, products).astype(jnp.int16)
    both_products = lax.all_gather(own_product, "pt", axis=0, tiled=True)
    first_product = both_products[: 2 * DEG]
    shifted = both_products[3 * DEG :]
    own_tables = [
        lax.dynamic_slice_in_dim(
            jnp.asarray(digit, dtype=jnp.bfloat16), place * half_points, half_points, 0
        )
        for digit in forward_two
    ]
    upper_values = centred_transform(*own_tables, first_product)
    lower_values = centred_transform(*[digit[:, :DEG] for digit in own_tables], shifted)
    products_two = column_pointwise(upper_values, lower_values)
    all_points = lax.all_to_all(products_two, "pt", split_axis=1, concat_axis=0, tiled=True)
    result = centred_transform(*inverse_two, all_points)
    return jnp.where(result < 0.0, result + 12289.0, result) / 12289.0


def centre(values):
    return jnp.where(values > modulus // 2, values - modulus, values)


def solution(mesh):
    in_specs = (P("pt", "row", "col"), P("pt", "row", "col"))
    out_specs = P(None, ("row", "pt"), "col")
    body = pair_local if mesh.shape["pt"] == 2 else local
    return jax.shard_map(body, mesh=mesh, in_specs=in_specs, out_specs=out_specs, check_vma=False)
```

profile of v0, /device:TPU:0, one launch (start us, length us, event | category | flops | bytes accessed | tf_op | source)
XLA Modules:
  0.0 1258.8 jit_solution(4259190581243966023)
XLA Ops:
  0.0 5.5 fusion.68
  6.8 1.4 fusion.55
  8.2 7.1 subtract_convert_fusion.8
  15.3 4.3 copy.69
  19.6 6.6 all-to-all-start
  26.2 5.4 fusion.67
  31.7 1.4 fusion.59
  34.3 7.1 subtract_convert_fusion.7
  41.4 4.4 copy.74
  45.8 73.8 %all-to-all-done = s16[32,256,256]{2,1,0:T(8,128)(2,1)} async-done(((s16[32,256,256]{2,1,0:T(8,128)(2,1)}), s16[32,256,256]{2,1,0:T(8,128)(2,1)}, u32[]{:S(2)}, u32[]{:S(2)}) %all-to-all-start) | async-done | bytes 4194336 | tf_op jit(solution)/shard_map/all_to_all | solution.py:211
  119.6 5.3 all-to-all-start.1
  124.9 6.8 convert.12
  131.8 12.0 copy.111
  143.8 10.8 reshape.16
  154.6 63.0 %all-to-all-done.1 = s16[32,256,256]{2,1,0:T(8,128)(2,1)} async-done(((s16[32,256,256]{2,1,0:T(8,128)(2,1)}), s16[32,256,256]{2,1,0:T(8,128)(2,1)}, u32[]{:S(2)}, u32[]{:S(2)}) %all-to-all-start.1) | async-done | bytes 4194336 | tf_op jit(solution)/shard_map/all_to_all | solution.py:207
  217.6 7.4 copy.113
  225.0 7.9 all_to_all.71
  232.9 105.4 %all-gather.3 = s16[8,1024,1024]{2,1,0:T(8,128)(2,1)} all-gather(s16[8,256,1024]{2,1,0:T(8,128)(2,1)} %all_to_all.71), channel_id=1, replica_groups=mesh['row'=4,'col'=4,'pt'=2] {'row'}, dimensions={1}, use_global_device_ids=true | all-gather | bytes 20971520 | tf_op jit(solution)/shard_map/all_gather | solution.py:210
  338.4 16.5 %fusion.14 = f32[8,256,1024]{2,1,0:T(8,128)} fusion(s16[8,1024,1024]{2,1,0:T(8,128)(2,1)} %all-gather.3, f32[8,256,1024]{2,1,0:T(8,128)} %reshape.16), kind=kOutput, calls=%fused_computation.16 | convolution fusion | flops 4334813184 | bytes 33554432 | tf_op jit(solution)/shard_map/bik,bkj->bij/dot_general | solution.py:74
  354.9 17.6 %fusion.12 = f32[8,256,1024]{2,1,0:T(8,128)} fusion(s16[8,1024,1024]{2,1,0:T(8,128)(2,1)} %all-gather.3, f32[8,256,1024]{2,1,0:T(8,128)} %reshape.16), kind=kOutput, calls=%fused_computation.15 | convolution fusion | flops 4339007488 | bytes 33554432 | tf_op jit(solution)/shard_map/bik,bkj->bij/dot_general | solution.py:74
  372.5 18.3 %fusion.20 = f32[8,256,1024]{2,1,0:T(8,128)} fusion(s16[8,1024,1024]{2,1,0:T(8,128)(2,1)} %all-gather.3, f32[8,256,1024]{2,1,0:T(8,128)} %reshape.16), kind=kOutput, calls=%fused_computation.23 | convolution fusion | flops 4355784704 | bytes 33554432 | tf_op jit(solution)/shard_map/bik,bkj->bij/dot_general | solution.py:74
  390.8 25.6 %subtract_convert_fusion.5 = s16[8,256,1024]{2,1,0:T(8,128)(2,1)} fusion(f32[8,256,1024]{2,1,0:T(8,128)} %fusion.20, f32[8,256,1024]{2,1,0:T(8,128)} %fusion.12, f32[8,256,1024]{2,1,0:T(8,128)} %fusion.14, s16[8,1024,1024]{2,1,0:T(8,128)(2,1)} %all-gather.3, f32[8,256,1024]{2,1,0:T(8,128)} %reshape.16), kind=kOutput, calls=%fused_computation.59 | convolution fusion | flops 4389339136 | bytes 54525952 | tf_op jit(solution)/shard_map/bik,bkj->bij/dot_general | solution.py:74
  416.3 7.3 copy.76
  423.6 5.1 all-to-all-start.2
  428.8 94.0 %all-to-all-done.2 = s16[8,256,1024]{1,0,2:T(8,128)(2,1)} async-done(((s16[8,256,1024]{1,0,2:T(8,128)(2,1)}), s16[8,256,1024]{1,0,2:T(8,128)(2,1)}, u32[]{:S(2)}, u32[]{:S(2)}) %all-to-all-start.2) | async-done | bytes 4194336 | tf_op jit(solution)/shard_map/all_to_all | solution.py:220
  522.8 6.5 convert.13
  529.3 10.5 copy.77
  539.8 4.5 fusion.46
  545.5 1.5 fusion.28
  547.0 8.1 subtract_convert_fusion.4
  555.1 92.8 %all-gather.4 = s16[64,256,256]{2,0,1:T(8,128)(2,1)S(1)} all-gather(s16[32,256,256]{2,0,1:T(8,128)(2,1)} %subtract_convert_fusion.4), channel_id=1, replica_groups=mesh['row'=4,'col'=4,'pt'=2] {'pt'}, dimensions={0}, use_global_device_ids=true | all-gather | bytes 12582912 | tf_op jit(solution)/shard_map/all_gather | solution.py:237
  648.0 3.1 fusion.27
  651.1 4.6 fusion.84
  657.1 10.0 subtract_convert_fusion.3
  667.0 4.3 copy.78
  671.3 5.1 all-to-all-start.3
  676.4 3.0 fusion.52
  682.9 8.5 subtract_convert_fusion.2
  691.5 6.5 copy.82
  698.0 70.7 %all-to-all-done.3 = s16[32,256,256]{2,1,0:T(8,128)(2,1)} async-done(((s16[32,256,256]{2,1,0:T(8,128)(2,1)}), s16[32,256,256]{2,1,0:T(8,128)(2,1)}, u32[]{:S(2)}, u32[]{:S(2)}) %all-to-all-start.3) | async-done | bytes 4194336 | tf_op jit(solution)/shard_map/all_to_all | solution.py:211
  768.7 5.1 all-to-all-start.4
  773.8 6.8 convert.14
  780.6 12.0 copy.110
  792.6 10.8 reshape.18
  803.4 63.1 %all-to-all-done.4 = s16[32,256,256]{2,1,0:T(8,128)(2,1)} async-done(((s16[32,256,256]{2,1,0:T(8,128)(2,1)}), s16[32,256,256]{2,1,0:T(8,128)(2,1)}, u32[]{:S(2)}, u32[]{:S(2)}) %all-to-all-start.4) | async-done | bytes 4194336 | tf_op jit(solution)/shard_map/all_to_all | solution.py:207
  866.5 7.4 copy.112
  874.0 7.9 all_to_all.77
  881.9 104.5 %all-gather.5 = s16[8,1024,1024]{2,1,0:T(8,128)(2,1)} all-gather(s16[8,256,1024]{2,1,0:T(8,128)(2,1)} %all_to_all.77), channel_id=1, replica_groups=mesh['row'=4,'col'=4,'pt'=2] {'row'}, dimensions={1}, use_global_device_ids=true | all-gather | bytes 20971520 | tf_op jit(solution)/shard_map/all_gather | solution.py:210
  986.4 16.5 %fusion.10 = f32[8,256,1024]{2,1,0:T(8,128)} fusion(s16[8,1024,1024]{2,1,0:T(8,128)(2,1)} %all-gather.5, f32[8,256,1024]{2,1,0:T(8,128)} %reshape.18), kind=kOutput, calls=%fused_computation.14 | convolution fusion | flops 4334813184 | bytes 33554432 | tf_op jit(solution)/shard_map/bik,bkj->bij/dot_general | solution.py:74
  1002.9 17.6 %fusion.8 = f32[8,256,1024]{2,1,0:T(8,128)} fusion(s16[8,1024,1024]{2,1,0:T(8,128)(2,1)} %all-gather.5, f32[8,256,1024]{2,1,0:T(8,128)} %reshape.18), kind=kOutput, calls=%fused_computation.13 | convolution fusion | flops 4339007488 | bytes 33554432 | tf_op jit(solution)/shard_map/bik,bkj->bij/dot_general | solution.py:74
  1020.5 18.3 %fusion.16 = f32[8,256,1024]{2,1,0:T(8,128)} fusion(s16[8,1024,1024]{2,1,0:T(8,128)(2,1)} %all-gather.5, f32[8,256,1024]{2,1,0:T(8,128)} %reshape.18), kind=kOutput, calls=%fused_computation.21 | convolution fusion | flops 4355784704 | bytes 33554432 | tf_op jit(solution)/shard_map/bik,bkj->bij/dot_general | solution.py:74
  1038.7 25.6 %subtract_convert_fusion = s16[8,256,1024]{2,1,0:T(8,128)(2,1)} fusion(f32[8,256,1024]{2,1,0:T(8,128)} %fusion.16, f32[8,256,1024]{2,1,0:T(8,128)} %fusion.8, f32[8,256,1024]{2,1,0:T(8,128)} %fusion.10, s16[8,1024,1024]{2,1,0:T(8,128)(2,1)} %all-gather.5, f32[8,256,1024]{2,1,0:T(8,128)} %reshape.18), kind=kOutput, calls=%fused_computation.52 | convolution fusion | flops 4389339136 | bytes 54525952 | tf_op jit(solution)/shard_map/bik,bkj->bij/dot_general | solution.py:74
  1064.3 7.3 copy.84
  1071.5 99.7 %all_to_all.90 = s16[8,256,1024]{1,0,2:T(8,128)(2,1)} all-to-all(s16[8,256,1024]{1,0,2:T(8,128)(2,1)} %copy.84), channel_id=1, replica_groups=mesh['row'=4,'col'=4,'pt'=2] {'col'}, dimensions={2} | all-to-all | bytes 8388608 | tf_op jit(solution)/shard_map/all_to_all | solution.py:220
  1171.2 7.9 copy.86
  1179.1 4.5 copy.87
  1183.6 50.0 %all_to_all.91 = s16[32,256,256]{2,0,1:T(8,128)(2,1)S(1)} all-to-all(s16[32,256,256]{2,0,1:T(8,128)(2,1)S(1)} %copy.87), channel_id=1, replica_groups=mesh['row'=4,'col'=4,'pt'=2] {'pt'}, dimensions={1} | all-to-all | bytes 8388608 | tf_op jit(solution)/shard_map/all_to_all | solution.py:249
  1233.6 2.4 copy.88
  1236.0 1.4 convert_bitcast_fusion
  1237.4 4.9 copy.89
  1242.3 2.1 fusion.41
  1245.4 1.5 fusion.36
  1246.9 5.5 fusion.48
  1252.4 6.0 copy.90
  (38 shorter events, 9.6 us)
Async XLA Ops:
  0.0 5.5 copy-start.3
  0.0 6.8 copy-start.2
  6.7 1.4 copy-start.11
  19.6 100.0 %all-to-all-start = ((s16[32,256,256]{2,1,0:T(8,128)(2,1)}), s16[32,256,256]{2,1,0:T(8,128)(2,1)}, u32[]{:S(2)}, u32[]{:S(2)}) async-start(s16[32,256,256]{2,1,0:T(8,128)(2,1)} %copy.69), calls=%async_computation | async-start | bytes 8388608 | tf_op jit(solution)/shard_map/all_to_all | solution.py:211
  119.6 98.0 %all-to-all-start.1 = ((s16[32,256,256]{2,1,0:T(8,128)(2,1)}), s16[32,256,256]{2,1,0:T(8,128)(2,1)}, u32[]{:S(2)}, u32[]{:S(2)}) async-start(s16[32,256,256]{2,1,0:T(8,128)(2,1)} %copy.74), calls=%async_computation.1 | async-start | bytes 8388608 | tf_op jit(solution)/shard_map/all_to_all | solution.py:207
  416.3 12.5 copy-start.1
  416.3 12.5 copy-start.4
  423.6 99.2 %all-to-all-start.2 = ((s16[8,256,1024]{1,0,2:T(8,128)(2,1)}), s16[8,256,1024]{1,0,2:T(8,128)(2,1)}, u32[]{:S(2)}, u32[]{:S(2)}) async-start(s16[8,256,1024]{1,0,2:T(8,128)(2,1)} %copy.76), calls=%async_computation.2 | async-start | bytes 8388608 | tf_op jit(solution)/shard_map/all_to_all | solution.py:220
  539.8 4.5 copy-start.8
  544.3 1.3 copy-start.7
  545.5 1.5 copy-start.10
  648.0 9.1 copy-start
  671.3 97.4 %all-to-all-start.3 = ((s16[32,256,256]{2,1,0:T(8,128)(2,1)}), s16[32,256,256]{2,1,0:T(8,128)(2,1)}, u32[]{:S(2)}, u32[]{:S(2)}) async-start(s16[32,256,256]{2,1,0:T(8,128)(2,1)} %copy.78), calls=%async_computation.3 | async-start | bytes 8388608 | tf_op jit(solution)/shard_map/all_to_all | solution.py:211
  676.4 4.3 slice-start
  679.4 2.2 slice-start.1
  768.7 97.8 %all-to-all-start.4 = ((s16[32,256,256]{2,1,0:T(8,128)(2,1)}), s16[32,256,256]{2,1,0:T(8,128)(2,1)}, u32[]{:S(2)}, u32[]{:S(2)}) async-start(s16[32,256,256]{2,1,0:T(8,128)(2,1)} %copy.82), calls=%async_computation.4 | async-start | bytes 8388608 | tf_op jit(solution)/shard_map/all_to_all | solution.py:207
  1242.3 2.2 copy-start.5
  1244.4 1.0 copy-start.6
  1245.4 1.5 copy-start.9
where the time goes:
time: 1270 us; the launch traced here: 1260 us
  blocking collectives  452 us (36%)
  waiting for transfers between devices  364 us (29%)
  matrix products  221 us (17%)
  local copies, waits for them, and re-layouts  148 us (12%)
  other arithmetic  45.2 us (4%)
  starting transfers between devices  27.2 us (2%)
    all_gather x2, blocking collectives, column_pointwise(): right_points = lax.all_gather(right_points, 'row', axis=1, tiled=True)  210 us
    dot_general x8, matrix products, batched_product(): jnp.einsum('bik,bkj->bij', left_part, right_part, preferred_element_type=...  156 us
    all_to_all x2, waiting for transfers between devices, column_pointwise(): lax.all_to_all(left_values.astype(jnp.int16), 'col', split_axis=0, concat...  144 us
    all_to_all x2, waiting for transfers between devices, column_pointwise(): lax.all_to_all(right_values.astype(jnp.int16), 'col', split_axis=0, conca...  126 us
    all_to_all x1, blocking collectives, column_pointwise(): lax.all_to_all(product_values.astype(jnp.int16), 'col', split_axis=2, con...  99.7 us
    all_to_all x1, waiting for transfers between devices, column_pointwise(): lax.all_to_all(product_values.astype(jnp.int16), 'col', split_axis=2, con...  94 us
    all_gather x1, blocking collectives, pair_local(): both_products = lax.all_gather(own_product, 'pt', axis=0, tiled=True)  92.8 us
    dot_general x18, matrix products, product_of(): jnp.einsum('ts,sab->tab', left_part, right_part, preferred_element_type=j...  65.3 us
  transfers between devices with their start and end apart: 5, of which 5 were waited for; matrix products, arithmetic and copies ran while one was open for 8% of the time, Pallas kernels for 0%

commit v1 on v0

--- a/solution.py
+++ b/solution.py
@@ -7,6 +7,18 @@
 DEG = 16
 modulus = 12289
 digit_base = 128
+
+
+def rotated_exchange(array, axis, split, join):
+    ways, here = (lax.axis_size(axis), lax.axis_index(axis))
+    width = array.shape[split] // ways
+    turned = jnp.roll(array, -here * width, axis=split)
+    got = [lax.slice_in_dim(turned, 0, width, axis=split)]
+    for far in range(1, ways):
+        sent = lax.slice_in_dim(turned, far * width, (far + 1) * width, axis=split)
+        got.append(lax.ppermute(sent, axis, [(d, (d + far) % ways) for d in range(ways)]))
+    line = jnp.concatenate(got[::-1], axis=join)
+    return jnp.roll(line, (here + 1) * got[0].shape[join], axis=join)
 
 
 def primitive_root():
@@ -208,9 +220,7 @@
         right_values.astype(jnp.int16), "col", split_axis=0, concat_axis=2, tiled=True
     )
     right_points = lax.all_gather(right_points, "row", axis=1, tiled=True)
-    left_points = lax.all_to_all(
-        left_values.astype(jnp.int16), "col", split_axis=0, concat_axis=2, tiled=True
-    )
+    left_points = rotated_exchange(left_values.astype(jnp.int16), "col", 0, 2)
     left_high, left_low = centred_digits(left_points.astype(jnp.float32))
     right_high, right_low = centred_digits(right_points.astype(jnp.float32))
     middle = batched_product(left_high, right_low) + batched_product(left_low, right_high)

time: 1270 us -> 1350 us (1.063)
  other arithmetic: 45.2 us -> 128 us
  local copies, waits for them, and re-layouts: 148 us -> 91.6 us
  waiting for transfers between devices: 364 us -> 407 us
    ppermute x0 -> x6, waiting for transfers between devices: none -> 313 us  [rotated_exchange(): lax.ppermute(sent, axis, [(d, (d + far) % ways) for d in range(ways)])]
    all_to_all x2 -> x0, waiting for transfers between devices: 144 us -> none  [column_pointwise(): lax.all_to_all(left_values.astype(jnp.int16), 'col', split_axis=0, concat...]
    all_to_all x2, waiting for transfers between devices: 126 us -> 0.01 us  [column_pointwise(): lax.all_to_all(right_values.astype(jnp.int16), 'col', split_axis=0, conca...]
    convert_element_type x6 -> x0, local copies, waits for them, and re-layouts: 54.3 us -> none  [the longest x4 45.7 us: column_pointwise(): left_high, left_low = centred_digits(left_points.astype(jnp.float32))]
    convert_element_type x2, other arithmetic: 13.6 us -> 66.9 us  [column_pointwise(): product_values.astype(jnp.int16)]
    convert_element_type x3 -> x5, other arithmetic: 15.4 us -> 32.1 us  [centred_digits(): high_digit.astype(jnp.bfloat16)]
  transfers between devices with their start and end apart: 5 -> 9, of which waited for: 5 -> 5; matrix products, arithmetic and copies ran while one was open for 8% -> 5% of each run, Pallas kernels for 0% -> 0%
where the time goes in v1:
time: 1350 us; the launch traced here: 1340 us
  blocking collectives  453 us (34%)
  waiting for transfers between devices  407 us (30%)
  matrix products  230 us (17%)
  other arithmetic  128 us (9%)
  local copies, waits for them, and re-layouts  91.6 us (7%)
  starting transfers between devices  26.7 us (2%)
    ppermute x6, waiting for transfers between devices, rotated_exchange(): lax.ppermute(sent, axis, [(d, (d + far) % ways) for d in range(ways)])  313 us
    all_gather x2, blocking collectives, column_pointwise(): right_points = lax.all_gather(right_points, 'row', axis=1, tiled=True)  210 us
    dot_general x8, matrix products, batched_product(): jnp.einsum('bik,bkj->bij', left_part, right_part, preferred_element_type=...  167 us
    all_to_all x1, blocking collectives, column_pointwise(): lax.all_to_all(product_values.astype(jnp.int16), 'col', split_axis=2, con...  99.7 us
    all_to_all x1, waiting for transfers between devices, column_pointwise(): lax.all_to_all(product_values.astype(jnp.int16), 'col', split_axis=2, con...  94 us
    all_gather x1, blocking collectives, pair_local(): both_products = lax.all_gather(own_product, 'pt', axis=0, tiled=True)  92.9 us
    convert_element_type x2, other arithmetic, column_pointwise(): product_values.astype(jnp.int16)  66.9 us
    dot_general x18, matrix products, product_of(): jnp.einsum('ts,sab->tab', left_part, right_part, preferred_element_type=j...  62.8 us
  transfers between devices with their start and end apart: 9, of which 5 were waited for; matrix products, arithmetic and copies ran while one was open for 5% of the time, Pallas kernels for 0%

profile of v1, /device:TPU:0, one launch (start us, length us, event | category | flops | bytes accessed | tf_op | source)
XLA Modules:
  0.0 1337.4 jit_solution(302708210319452011)
XLA Ops:
  0.0 5.5 fusion.91
  6.8 1.4 fusion.83
  8.2 7.1 subtract_convert_fusion.5
  15.3 4.4 copy.116
  19.7 6.5 all-to-all-start
  26.2 5.4 fusion.92
  31.7 1.4 fusion.79
  34.4 7.1 subtract_convert_fusion.6
  41.4 2.3 fusion.76
  43.7 1.9 fusion.136
  45.6 3.8 collective-permute-start
  50.8 66.8 %collective-permute-done = s16[8,256,256]{2,0,1:T(8,128)(2,1)S(1)} collective-permute-done((s16[8,256,256]{2,0,1:T(8,128)(2,1)}, s16[8,256,256]{2,0,1:T(8,128)(2,1)S(1)}, u32[]{:S(2)}, u32[]{:S(2)}) %collective-permute-start) | collective-permute-done | bytes 1048608 | tf_op jit(solution)/shard_map/ppermute | solution.py:19
  117.5 91.9 %collective-permute-done.1 = s16[8,256,256]{2,0,1:T(8,128)(2,1)S(1)} collective-permute-done((s16[8,256,256]{2,0,1:T(8,128)(2,1)}, s16[8,256,256]{2,0,1:T(8,128)(2,1)S(1)}, u32[]{:S(2)}, u32[]{:S(2)}) %collective-permute-start.1) | collective-permute-done | bytes 1048608 | tf_op jit(solution)/shard_map/ppermute | solution.py:19
  209.4 8.7 fusion.26
  218.1 3.7 fusion.27
  221.8 7.4 copy.204
  229.3 7.8 all_to_all.56
  237.1 105.3 %all-gather.3 = s16[8,1024,1024]{2,1,0:T(8,128)(2,1)} all-gather(s16[8,256,1024]{2,1,0:T(8,128)(2,1)} %all_to_all.56), channel_id=1, replica_groups=mesh['row'=4,'col'=4,'pt'=2] {'row'}, dimensions={1}, use_global_device_ids=true | all-gather | bytes 20971520 | tf_op jit(solution)/shard_map/all_gather | solution.py:222
  342.4 18.7 %fusion.14 = f32[8,256,1024]{2,1,0:T(8,128)S(1)} fusion(s16[8,1024,1024]{2,1,0:T(8,128)(2,1)} %all-gather.3, bf16[8,256,1024]{2,0,1:T(8,128)(2,1)} %get-tuple-element.9), kind=kOutput, calls=%fused_computation.16 | convolution fusion | flops 4328521728 | bytes 29360128 | tf_op jit(solution)/shard_map/bik,bkj->bij/dot_general | solution.py:86
  361.1 22.1 %fusion.22 = f32[8,256,1024]{2,1,0:T(8,128)} fusion(s16[8,1024,1024]{2,1,0:T(8,128)(2,1)} %all-gather.3, bf16[8,256,1024]{2,0,1:T(8,128)(2,1)} %get-tuple-element.9), kind=kOutput, calls=%fused_computation.28 | convolution fusion | flops 4345298944 | bytes 29360128 | tf_op jit(solution)/shard_map/bik,bkj->bij/dot_general | solution.py:86
  383.3 20.8 %fusion.12 = f32[8,256,1024]{2,1,0:T(8,128)} fusion(s16[8,1024,1024]{2,1,0:T(8,128)(2,1)} %all-gather.3, bf16[8,256,1024]{2,0,1:T(8,128)(2,1)} %fusion.27), kind=kOutput, calls=%fused_computation.15 | convolution fusion | flops 4328521728 | bytes 29360128 | tf_op jit(solution)/shard_map/bik,bkj->bij/dot_general | solution.py:86
  404.1 21.8 %fusion.20 = f32[8,256,1024]{2,1,0:T(8,128)} fusion(s16[8,1024,1024]{2,1,0:T(8,128)(2,1)} %all-gather.3, bf16[8,256,1024]{2,0,1:T(8,128)(2,1)} %fusion.27), kind=kOutput, calls=%fused_computation.27 | convolution fusion | flops 4345298944 | bytes 29360128 | tf_op jit(solution)/shard_map/bik,bkj->bij/dot_general | solution.py:86
  425.9 33.4 %subtract_convert_fusion.4 = s16[8,256,1024]{2,0,1:T(8,128)(2,1)} fusion(f32[8,256,1024]{2,1,0:T(8,128)} %fusion.20, f32[8,256,1024]{2,1,0:T(8,128)} %fusion.12, f32[8,256,1024]{2,1,0:T(8,128)} %fusion.22, f32[8,256,1024]{2,1,0:T(8,128)S(1)} %fusion.14), kind=kLoop, calls=%fused_computation.92 | loop fusion | flops 37748736 | bytes 37748736 | tf_op jit(solution)/shard_map/convert_element_type | solution.py:231
  459.2 7.4 copy.127
  466.6 5.3 all-to-all-start.1
  472.0 94.0 %all-to-all-done.1 = s16[8,256,1024]{1,0,2:T(8,128)(2,1)} async-done(((s16[8,256,1024]{1,0,2:T(8,128)(2,1)}), s16[8,256,1024]{1,0,2:T(8,128)(2,1)}, u32[]{:S(2)}, u32[]{:S(2)}) %all-to-all-start.1) | async-done | bytes 4194336 | tf_op jit(solution)/shard_map/all_to_all | solution.py:230
  566.0 6.6 convert.6
  572.5 10.5 copy.128
  583.0 4.5 fusion.54
  588.8 1.5 fusion.36
  590.3 8.1 subtract_convert_fusion.3
  598.4 92.9 %all-gather.4 = s16[64,256,256]{2,0,1:T(8,128)(2,1)S(1)} all-gather(s16[32,256,256]{2,0,1:T(8,128)(2,1)} %subtract_convert_fusion.3), channel_id=1, replica_groups=mesh['row'=4,'col'=4,'pt'=2] {'pt'}, dimensions={0}, use_global_device_ids=true | all-gather | bytes 12582912 | tf_op jit(solution)/shard_map/all_gather | solution.py:247
  695.1 8.7 subtract_convert_fusion.1
  703.8 6.6 copy.131
  710.4 4.8 all-to-all-start.2
  715.3 4.4 fusion.31
  719.7 1.3 fusion.40
  721.9 2.6 fusion.108
  724.5 9.3 subtract_convert_fusion.2
  733.8 3.6 fusion.68
  737.7 3.8 collective-permute-start.3
  742.6 63.9 %collective-permute-done.3 = s16[8,256,256]{2,0,1:T(8,128)(2,1)S(1)} collective-permute-done((s16[8,256,256]{2,0,1:T(8,128)(2,1)S(1)}, s16[8,256,256]{2,0,1:T(8,128)(2,1)S(1)}, u32[]{:S(2)}, u32[]{:S(2)}) %collective-permute-start.3) | collective-permute-done | bytes 1048608 | tf_op jit(solution)/shard_map/ppermute | solution.py:19
  806.5 90.8 %collective-permute-done.4 = s16[8,256,256]{2,0,1:T(8,128)(2,1)S(1)} collective-permute-done((s16[8,256,256]{2,0,1:T(8,128)(2,1)S(1)}, s16[8,256,256]{2,0,1:T(8,128)(2,1)S(1)}, u32[]{:S(2)}, u32[]{:S(2)}) %collective-permute-start.4) | collective-permute-done | bytes 1048608 | tf_op jit(solution)/shard_map/ppermute | solution.py:19
  897.3 8.1 fusion.34
  905.4 3.7 fusion.35
  909.1 7.4 copy.203
  916.6 7.8 all_to_all.61
  924.4 104.2 %all-gather.5 = s16[8,1024,1024]{2,1,0:T(8,128)(2,1)} all-gather(s16[8,256,1024]{2,1,0:T(8,128)(2,1)} %all_to_all.61), channel_id=1, replica_groups=mesh['row'=4,'col'=4,'pt'=2] {'row'}, dimensions={1}, use_global_device_ids=true | all-gather | bytes 20971520 | tf_op jit(solution)/shard_map/all_gather | solution.py:222
  1028.6 18.7 %fusion.10 = f32[8,256,1024]{2,1,0:T(8,128)S(1)} fusion(s16[8,1024,1024]{2,1,0:T(8,128)(2,1)} %all-gather.5, bf16[8,256,1024]{2,0,1:T(8,128)(2,1)} %get-tuple-element.6), kind=kOutput, calls=%fused_computation.14 | convolution fusion | flops 4328521728 | bytes 29360128 | tf_op jit(solution)/shard_map/bik,bkj->bij/dot_general | solution.py:86
  1047.3 22.1 %fusion.18 = f32[8,256,1024]{2,1,0:T(8,128)} fusion(s16[8,1024,1024]{2,1,0:T(8,128)(2,1)} %all-gather.5, bf16[8,256,1024]{2,0,1:T(8,128)(2,1)} %get-tuple-element.6), kind=kOutput, calls=%fused_computation.26 | convolution fusion | flops 4345298944 | bytes 29360128 | tf_op jit(solution)/shard_map/bik,bkj->bij/dot_general | solution.py:86
  1069.4 20.8 %fusion.8 = f32[8,256,1024]{2,1,0:T(8,128)} fusion(s16[8,1024,1024]{2,1,0:T(8,128)(2,1)} %all-gather.5, bf16[8,256,1024]{2,0,1:T(8,128)(2,1)} %fusion.35), kind=kOutput, calls=%fused_computation.13 | convolution fusion | flops 4328521728 | bytes 29360128 | tf_op jit(solution)/shard_map/bik,bkj->bij/dot_general | solution.py:86
  1090.3 21.8 %fusion.16 = f32[8,256,1024]{2,1,0:T(8,128)} fusion(s16[8,1024,1024]{2,1,0:T(8,128)(2,1)} %all-gather.5, bf16[8,256,1024]{2,0,1:T(8,128)(2,1)} %fusion.35), kind=kOutput, calls=%fused_computation.25 | convolution fusion | flops 4345298944 | bytes 29360128 | tf_op jit(solution)/shard_map/bik,bkj->bij/dot_general | solution.py:86
  1112.0 33.5 %subtract_convert_fusion = s16[8,256,1024]{2,0,1:T(8,128)(2,1)} fusion(f32[8,256,1024]{2,1,0:T(8,128)} %fusion.16, f32[8,256,1024]{2,1,0:T(8,128)} %fusion.8, f32[8,256,1024]{2,1,0:T(8,128)} %fusion.18, f32[8,256,1024]{2,1,0:T(8,128)S(1)} %fusion.10), kind=kLoop, calls=%fused_computation.88 | loop fusion | flops 37748736 | bytes 37748736 | tf_op jit(solution)/shard_map/convert_element_type | solution.py:231
  1145.6 7.4 copy.142
  1152.9 99.7 %all_to_all.72 = s16[8,256,1024]{1,0,2:T(8,128)(2,1)} all-to-all(s16[8,256,1024]{1,0,2:T(8,128)(2,1)} %copy.142), channel_id=1, replica_groups=mesh['row'=4,'col'=4,'pt'=2] {'col'}, dimensions={2} | all-to-all | bytes 8388608 | tf_op jit(solution)/shard_map/all_to_all | solution.py:230
  1252.6 8.6 copy.143
  1261.2 51.3 %all_to_all.73 = s16[32,256,256]{2,0,1:T(8,128)(2,1)S(1)} all-to-all(s16[32,256,256]{2,0,1:T(8,128)(2,1)} %bitcast.95), channel_id=1, replica_groups=mesh['row'=4,'col'=4,'pt'=2] {'pt'}, dimensions={1} | all-to-all | bytes 8388608 | tf_op jit(solution)/shard_map/all_to_all | solution.py:259
  1312.5 2.4 copy.144
  1314.9 1.4 convert_bitcast_fusion
  1316.3 4.9 copy.145
  1321.1 2.1 fusion.49
  1324.3 1.5 fusion.44
  1325.8 5.4 fusion.56
  1331.2 6.0 copy.146
  (47 shorter events, 12.3 us)
Async XLA Ops:
  0.0 5.5 copy-start.3
  0.0 6.8 copy-start.2
  6.7 1.4 copy-start.11
  19.7 202.2 %all-to-all-start = ((s16[32,256,256]{2,1,0:T(8,128)(2,1)}), s16[32,256,256]{2,1,0:T(8,128)(2,1)}, u32[]{:S(2)}, u32[]{:S(2)}) async-start(s16[32,256,256]{2,1,0:T(8,128)(2,1)} %copy.116), calls=%async_computation | async-start | bytes 8388608 | tf_op jit(solution)/shard_map/all_to_all | solution.py:219
  45.6 72.0 %collective-permute-start = (s16[8,256,256]{2,0,1:T(8,128)(2,1)}, s16[8,256,256]{2,0,1:T(8,128)(2,1)S(1)}, u32[]{:S(2)}, u32[]{:S(2)}) collective-permute-start(s16[8,256,256]{2,0,1:T(8,128)(2,1)} %get-tuple-element.23), channel_id=1, source_target_pairs={{0,6},{2,0},{4,2},{6,4},{1,7},{3,1},{5,3},{7,5},{8,14},{10,8},{12,... | collective-permute-start | bytes 3145736 | tf_op jit(solution)/shard_map/ppermute | solution.py:19
  49.4 160.0 %collective-permute-start.1 = (s16[8,256,256]{2,0,1:T(8,128)(2,1)}, s16[8,256,256]{2,0,1:T(8,128)(2,1)S(1)}, u32[]{:S(2)}, u32[]{:S(2)}) collective-permute-start(s16[8,256,256]{2,0,1:T(8,128)(2,1)} %get-tuple-element.25), channel_id=1, source_target_pairs={{0,4},{2,6},{4,0},{6,2},{1,5},{3,7},{5,1},{7,3},{8,12},{10,14},{12... | collective-permute-start | bytes 3145736 | tf_op jit(solution)/shard_map/ppermute | solution.py:19
  49.4 160.0 %collective-permute-start.2 = (s16[8,256,256]{2,0,1:T(8,128)(2,1)}, s16[8,256,256]{2,0,1:T(8,128)(2,1)}, u32[]{:S(2)}, u32[]{:S(2)}) collective-permute-start(s16[8,256,256]{2,0,1:T(8,128)(2,1)} %get-tuple-element.24), channel_id=1, source_target_pairs={{0,2},{2,4},{4,6},{6,0},{1,3},{3,5},{5,7},{7,1},{8,10},{10,12},{12... | collective-permute-start | bytes 3145736 | tf_op jit(solution)/shard_map/ppermute | solution.py:19
  459.2 12.8 copy-start.1
  459.2 12.8 copy-start.4
  466.6 99.3 %all-to-all-start.1 = ((s16[8,256,1024]{1,0,2:T(8,128)(2,1)}), s16[8,256,1024]{1,0,2:T(8,128)(2,1)}, u32[]{:S(2)}, u32[]{:S(2)}) async-start(s16[8,256,1024]{1,0,2:T(8,128)(2,1)} %copy.127), calls=%async_computation.1 | async-start | bytes 8388608 | tf_op jit(solution)/shard_map/all_to_all | solution.py:230
  583.0 4.5 copy-start.8
  587.5 1.3 copy-start.7
  588.8 1.5 copy-start.10
  691.2 3.9 copy-start
  710.4 198.7 %all-to-all-start.2 = ((s16[32,256,256]{2,1,0:T(8,128)(2,1)}), s16[32,256,256]{2,1,0:T(8,128)(2,1)}, u32[]{:S(2)}, u32[]{:S(2)}) async-start(s16[32,256,256]{2,1,0:T(8,128)(2,1)} %copy.131), calls=%async_computation.2 | async-start | bytes 8388608 | tf_op jit(solution)/shard_map/all_to_all | solution.py:219
  715.3 5.8 slice-start
  719.7 2.2 slice-start.1
  737.7 68.8 %collective-permute-start.3 = (s16[8,256,256]{2,0,1:T(8,128)(2,1)S(1)}, s16[8,256,256]{2,0,1:T(8,128)(2,1)S(1)}, u32[]{:S(2)}, u32[]{:S(2)}) collective-permute-start(s16[8,256,256]{2,0,1:T(8,128)(2,1)S(1)} %get-tuple-element.19), channel_id=1, source_target_pairs={{0,6},{2,0},{4,2},{6,4},{1,7},{3,1},{5,3},{7,5},{8,14},{10,8},{12,... | collective-permute-start | bytes 3145736 | tf_op jit(solution)/shard_map/ppermute | solution.py:19
  741.5 155.8 %collective-permute-start.4 = (s16[8,256,256]{2,0,1:T(8,128)(2,1)S(1)}, s16[8,256,256]{2,0,1:T(8,128)(2,1)S(1)}, u32[]{:S(2)}, u32[]{:S(2)}) collective-permute-start(s16[8,256,256]{2,0,1:T(8,128)(2,1)S(1)} %get-tuple-element.21), channel_id=1, source_target_pairs={{0,4},{2,6},{4,0},{6,2},{1,5},{3,7},{5,1},{7,3},{8,12},{10,14},{12... | collective-permute-start | bytes 3145736 | tf_op jit(solution)/shard_map/ppermute | solution.py:19
  741.5 155.8 %collective-permute-start.5 = (s16[8,256,256]{2,0,1:T(8,128)(2,1)S(1)}, s16[8,256,256]{2,0,1:T(8,128)(2,1)S(1)}, u32[]{:S(2)}, u32[]{:S(2)}) collective-permute-start(s16[8,256,256]{2,0,1:T(8,128)(2,1)S(1)} %get-tuple-element.20), channel_id=1, source_target_pairs={{0,2},{2,4},{4,6},{6,0},{1,3},{3,5},{5,7},{7,1},{8,10},{10,12},{12... | collective-permute-start | bytes 3145736 | tf_op jit(solution)/shard_map/ppermute | solution.py:19
  1321.1 2.2 copy-start.5
  1323.3 1.0 copy-start.6
  1324.3 1.5 copy-start.9
